TPU v7x, 32 devices: a whole 2x2x4 slice. The times are simulated.
32 devices in a mesh: blk: 8 (over y, x, core), uly: 4 (over z).
Axes of the slice: x: 2, y: 2, z: 4, core: 2. Of those that a mesh axis runs over, the one named last changes fastest.
Arguments:
- qkv: bfloat16 [2048, 3, 3072], P(('blk', 'uly')), may hold values from -9 to 9
Outputs:
- attended: float32 [2048, 3072], P('blk', 'uly')
- log_total: float32 [24, 2048], P('uly', 'blk')
All inputs are finite; a program needn't handle non-finite values.
Results may differ from a plain program's by a relative error of at most 0.0027.
Values may be sent and summed in bfloat16 or wider, within the bound.
No kernel may reach another device: no remote copies, remote signals or barrier semaphores. Data moves between devices by JAX's collectives and lax.ppermute only.
A program may use at most 64 MiB of HBM per device.

v0:
```python
import math
import jax
import jax.numpy as jnp
from jax import lax
from jax.sharding import PartitionSpec as P

HEAD_DIM = 128


def from_behind(value, axis, steps):
    count = lax.axis_size(axis)
    pairs = [(source, (source + steps) % count) for source in range(count)]
    return lax.ppermute(value, axis, pairs)


def block_scores(query_rows, key_rows, temper):
    return (
        jnp.einsum("rhd,khd->hrk", query_rows, key_rows, preferred_element_type=jnp.float32)
        * temper
    )


def attend_first(query_rows, key_rows, value_rows, temper):
    scores = block_scores(query_rows, key_rows, temper)
    top = jnp.max(scores, axis=2)
    weights = jnp.exp(scores - top[:, :, None])
    total = jnp.sum(weights, axis=2)
    accum = jnp.einsum(
        "hrk,khd->hrd", weights.astype(jnp.bfloat16), value_rows, preferred_element_type=jnp.float32
    )
    return (top, total, accum)


def attend_next(running, query_rows, key_rows, value_rows, temper):
    top, total, accum = running
    scores = block_scores(query_rows, key_rows, temper)
    newtop = jnp.maximum(top, jnp.max(scores, axis=2))
    factor = jnp.exp(top - newtop)
    weights = jnp.exp(scores - newtop[:, :, None])
    total = total * factor + jnp.sum(weights, axis=2)
    accum = accum * factor[:, :, None] + jnp.einsum(
        "hrk,khd->hrd", weights.astype(jnp.bfloat16), value_rows, preferred_element_type=jnp.float32
    )
    return (newtop, total, accum)


def shards(qkv):
    width = qkv.shape[2] // lax.axis_size("uly")
    heads_local = width // HEAD_DIM
    temper = 1.0 / math.sqrt(HEAD_DIM)
    grouped = lax.all_to_all(qkv, "uly", split_axis=2, concat_axis=0, tiled=True)
    prev_pairs = from_behind(grouped[:, 1:], "blk", 1)
    block_len = grouped.shape[0]
    row_count = math.gcd(block_len, 512)
    queries = grouped[:, 0].reshape(block_len // row_count, row_count, heads_local, HEAD_DIM)
    own_keys = grouped[:, 1].reshape(block_len, heads_local, HEAD_DIM)
    own_values = grouped[:, 2].reshape(block_len, heads_local, HEAD_DIM)
    prev_keys = prev_pairs[:, 0].reshape(block_len, heads_local, HEAD_DIM)
    prev_values = prev_pairs[:, 1].reshape(block_len, heads_local, HEAD_DIM)

    def per_rows(query_rows):
        running = attend_first(query_rows, own_keys, own_values, temper)
        top, total, accum = attend_next(running, query_rows, prev_keys, prev_values, temper)
        normed = accum / total[:, :, None]
        return (jnp.transpose(normed, (1, 0, 2)).reshape(row_count, width), top + jnp.log(total))

    attended_rows, log_rows = lax.map(per_rows, queries)
    attended = attended_rows.reshape(block_len, width)
    log_total = jnp.transpose(log_rows, (1, 0, 2)).reshape(heads_local, block_len)
    return (attended, log_total)


def solution(mesh):
    placed = (P(("blk", "uly"), None, None),)
    return jax.shard_map(
        shards,
        mesh=mesh,
        in_specs=placed,
        out_specs=(P("blk", "uly"), P("uly", "blk")),
        check_vma=False,
    )
```

profile of v0, /device:TPU:0, one launch (start us, length us, event | category | flops | bytes accessed | tf_op | source)
XLA Modules:
  0.0 74.6 jit_solution(17815620228269308837)
XLA Ops:
  0.6 4.6 %copy.32 = bf16[64,3,3072]{0,1,2:T(4,128)(2,1)S(1)} copy(bf16[64,3,3072]{2,0,1:T(8,128)(2,1)} %param.1) | data formatting | bytes 2359296 | tf_op args[0]
  5.2 3.1 %reshape.40 = bf16[4,2,73728]{2,1,0:T(2,128)(2,1)} reshape(bf16[3072,3,64]{2,1,0:T(4,128)(2,1)S(1)} %bitcast.42) | data formatting | bytes 2359296
  8.3 35.0 %all_to_all.18 = bf16[4,2,73728]{2,1,0:T(2,128)(2,1)} all-to-all(bf16[4,2,73728]{2,1,0:T(2,128)(2,1)} %reshape.40), channel_id=1, replica_groups=mesh['blk'=8,'uly'=4] {'uly'}, dimensions={0} | all-to-all | bytes 2359296 | tf_op jit(solution)/shard_map/all_to_all | solution.py:51
  43.2 3.5 %reshape.41 = bf16[3072,3,64]{2,1,0:T(4,128)(2,1)S(1)} reshape(bf16[4,2,73728]{2,1,0:T(2,128)(2,1)} %all_to_all.18) | data formatting | bytes 2359296
  46.7 3.2 %copy.34 = bf16[4,64,3,768]{3,1,0,2:T(8,128)(2,1)} copy(bf16[4,64,3,768]{1,2,3,0:T(4,128)(2,1)S(1)} %bitcast.41) | data formatting | bytes 2359296 | tf_op jit(solution)/shard_map/all_to_all | solution.py:51
  49.9 0.0 copy-start
  49.9 2.2 %slice.27 = bf16[256,2,768]{2,0,1:T(8,128)(2,1)} slice(bf16[256,3,768]{2,0,1:T(8,128)(2,1)} %bitcast.43), slice={[0:256], [1:3], [0:768]} | slice | bytes 1572864 | tf_op jit(solution)/shard_map/slice | solution.py:52
  52.1 0.0 collective-permute-start
  52.1 0.0 copy-done
  52.1 0.1 fusion.13
  52.2 0.2 copy.36
  52.3 0.9 %copy.39 = bf16[256,1,768]{0,2,1:T(8,128)(2,1)} copy(bf16[256,1,768]{2,0,1:T(8,128)(2,1)S(1)} %get-tuple-element.37) | data formatting | bytes 786432 | tf_op jit(solution)/shard_map/slice | solution.py:57
  53.2 0.2 copy.35
  53.4 0.4 fusion.15
  53.8 10.9 %collective-permute-done = bf16[256,2,768]{2,0,1:T(8,128)(2,1)} collective-permute-done((bf16[256,2,768]{2,0,1:T(8,128)(2,1)}, bf16[256,2,768]{2,0,1:T(8,128)(2,1)}, u32[]{:S(2)}, u32[]{:S(2)}) %collective-permute-start) | collective-permute-done | bytes 786464 | tf_op jit(solution)/shard_map/ppermute | solution.py:13
  64.7 1.9 %fusion.14 = (bf16[256,1,768]{2,0,1:T(8,128)(2,1)}, bf16[256,1,768]{2,0,1:T(8,128)(2,1)S(1)}) fusion(bf16[256,2,768]{2,0,1:T(8,128)(2,1)} %collective-permute-done), kind=kLoop, calls=%fused_computation.21 | loop fusion | bytes 1572864 | tf_op jit(solution)/shard_map/slice | solution.py:59
  66.6 0.9 %copy.41 = bf16[256,1,768]{0,2,1:T(8,128)(2,1)} copy(bf16[256,1,768]{2,0,1:T(8,128)(2,1)S(1)} %get-tuple-element.40) | data formatting | bytes 786432 | tf_op jit(solution)/shard_map/slice | solution.py:58
  67.5 1.4 %fusion.16 = (f32[6,256]{1,0:T(8,128)S(1)}, f32[6,256,256]{1,2,0:T(8,128)S(1)}) fusion(bf16[256,6,128]{0,2,1:T(8,128)(2,1)S(1)} %bitcast.46, bf16[256,6,128]{0,2,1:T(8,128)(2,1)} %bitcast.48), kind=kOutput, calls=%fused_computation.23 | convolution fusion | flops 101448192 | bytes 2365440 | tf_op jit(solution)/shard_map/while/body/eval_jaxpr/rhd,khd->hrk/dot_general | solution.py:18
  69.0 0.0 copy-start.1
  69.0 0.4 fusion
  69.4 0.6 log_add_fusion
  70.0 0.6 bitcast_add_fusion
  70.7 0.0 copy-done.1
  70.7 0.9 %copy.44 = bf16[256,1,768]{0,2,1:T(8,128)(2,1)} copy(bf16[256,1,768]{2,0,1:T(8,128)(2,1)S(1)} %copy-done.1) | data formatting | bytes 786432 | tf_op jit(solution)/shard_map/slice | solution.py:59
  71.6 0.0 copy-start.2
  71.6 0.0 copy-start.3
  71.6 1.5 %fusion.4 = f32[256,6,128]{0,2,1:T(8,128)S(1)} fusion(bf16[256,6,128]{0,2,1:T(8,128)(2,1)} %bitcast.49, f32[6,256,256]{1,2,0:T(8,128)S(1)} %get-tuple-element.42, f32[6,256]{1,0:T(8,128)S(1)} %get-tuple-element.41, f32[256,6]{0,1:T(8,128)} %get-tuple-element.35), kind=kOutput, calls=%fused_computation.10 | convolution fusion | flops 101646336 | bytes 2764800 | tf_op jit(solution)/shard_map/while/body/eval_jaxpr/hrk,khd->hrd/dot_general | solution.py:28
  73.0 0.0 copy-done.2
  73.0 0.0 copy-done.3
  73.1 0.4 fusion.6
  73.5 1.1 %copy.46 = f32[256,768]{1,0:T(8,128)} copy(f32[256,768]{0,1:T(8,128)S(1)} %bitcast.50) | data formatting | bytes 1572864
  (1 shorter events, 0.0 us)
Async XLA Ops:
  49.9 2.2 %copy-start = (bf16[4,64,3,768]{3,1,0,2:T(8,128)(2,1)S(1)}, bf16[4,64,3,768]{3,1,0,2:T(8,128)(2,1)}, u32[]{:S(2)}) copy-start(bf16[4,64,3,768]{3,1,0,2:T(8,128)(2,1)} %copy.34) | copy-start | bytes 3538948
  52.1 12.6 %collective-permute-start = (bf16[256,2,768]{2,0,1:T(8,128)(2,1)}, bf16[256,2,768]{2,0,1:T(8,128)(2,1)}, u32[]{:S(2)}, u32[]{:S(2)}) collective-permute-start(bf16[256,2,768]{2,0,1:T(8,128)(2,1)} %slice.27), channel_id=1, source_target_pairs={{0,4},{4,8},{8,12},{12,16},{16,20},{20,24},{24,28},{28,0},{1,5},{5... | collective-permute-start | bytes 2359304 | tf_op jit(solution)/shard_map/ppermute | solution.py:13
  69.0 1.7 %copy-start.1 = (bf16[256,1,768]{2,0,1:T(8,128)(2,1)S(1)}, bf16[256,1,768]{2,0,1:T(8,128)(2,1)}, u32[]{:S(2)}) copy-start(bf16[256,1,768]{2,0,1:T(8,128)(2,1)} %get-tuple-element.39) | copy-start | bytes 1179652
  71.6 1.5 %copy-start.2 = (bf16[256,1,768]{0,2,1:T(8,128)(2,1)S(1)}, bf16[256,1,768]{0,2,1:T(8,128)(2,1)}, u32[]{:S(2)}) copy-start(bf16[256,1,768]{0,2,1:T(8,128)(2,1)} %copy.44) | copy-start | bytes 1179652
  71.6 1.5 %copy-start.3 = (f32[256,6]{0,1:T(8,128)S(1)}, f32[256,6]{0,1:T(8,128)}, u32[]{:S(2)}) copy-start(f32[256,6]{0,1:T(8,128)} %get-tuple-element.34) | copy-start | bytes 18436
where the time goes:
time: 75 us; the launch traced here: 74.6 us
  blocking collectives  35 us (47%)
  local copies, waits for them, and re-layouts  22.7 us (30%)
  waiting for transfers between devices  10.9 us (15%)
  matrix products  3.71 us (5%)
  other arithmetic  1.68 us (2%)
    all_to_all x1, blocking collectives, shards(): lax.all_to_all(qkv, 'uly', split_axis=2, concat_axis=0, tiled=True)  35 us
    unnamed x12, local copies, waits for them, and re-layouts  12.3 us
    ppermute x1, waiting for transfers between devices, from_behind(): return lax.ppermute(value, axis, pairs)  10.9 us
    all_to_all x1, local copies, waits for them, and re-layouts, shards(): lax.all_to_all(qkv, 'uly', split_axis=2, concat_axis=0, tiled=True)  3.21 us
    slice x2, local copies, waits for them, and re-layouts, shards(): prev_values = prev_pairs[:, 1].reshape(block_len, heads_local, HEAD_DIM)  2.83 us
    slice x1, local copies, waits for them, and re-layouts, shards(): prev_pairs = from_behind(grouped[:, 1:], 'blk', 1)  2.16 us
    dot_general x2, matrix products, block_scores(): jnp.einsum('rhd,khd->hrk', query_rows, key_rows, preferred_element_type=j...  1.84 us
  transfers between devices with their start and end apart: 1, of which 1 were waited for; matrix products, arithmetic and copies ran while one was open for 2% of the time, Pallas kernels for 0%

commit v1 on v0

--- a/solution.py
+++ b/solution.py
@@ -1,3 +1,4 @@
+import functools
 import math
 import jax
 import jax.numpy as jnp
@@ -5,6 +6,24 @@
 from jax.sharding import PartitionSpec as P
 
 HEAD_DIM = 128
+
+
+def finish_the_results(message, axis_name):
+    arr_out, formed = (lax.psum(1, axis_name), lax.axis_index(axis_name))
+    v_next = message.shape[2] // arr_out
+    y = jnp.roll(message, -formed * v_next, 2)
+    leaves = [lax.slice_in_dim(y, 0, v_next, axis=2)]
+    for i0 in range(1, arr_out):
+        s_next = lax.slice_in_dim(y, i0 * v_next, (i0 + 1) * v_next, axis=2)
+        leaves.append(
+            lax.ppermute(s_next, axis_name, [(pp, (pp + i0) % arr_out) for pp in range(arr_out)])
+        )
+    return jnp.roll(
+        jnp.concatenate(leaves[::-1], axis=0), (formed + 1) * leaves[0].shape[0], axis=0
+    )
+
+
+finish_the_tiles = functools.partial(finish_the_results, axis_name="uly")
 
 
 def from_behind(value, axis, steps):
@@ -48,7 +67,7 @@
     width = qkv.shape[2] // lax.axis_size("uly")
     heads_local = width // HEAD_DIM
     temper = 1.0 / math.sqrt(HEAD_DIM)
-    grouped = lax.all_to_all(qkv, "uly", split_axis=2, concat_axis=0, tiled=True)
+    grouped = finish_the_tiles(qkv)
     prev_pairs = from_behind(grouped[:, 1:], "blk", 1)
     block_len = grouped.shape[0]
     row_count = math.gcd(block_len, 512)

time: 75 us -> 62.8 us (0.84)
  blocking collectives: 35 us -> 0 us
  waiting for transfers between devices: 10.9 us -> 34.8 us
  local copies, waits for them, and re-layouts: 22.7 us -> 14.9 us
  starting transfers between devices: 0.01 us -> 6.23 us
  other arithmetic: 1.68 us -> 4.07 us
  matrix products: 3.71 us -> 1.67 us
    all_to_all x1 -> x0, blocking collectives: 35 us -> none  [shards(): lax.all_to_all(qkv, 'uly', split_axis=2, concat_axis=0, tiled=True)]
    ppermute x0 -> x3, waiting for transfers between devices: none -> 23.2 us  [finish_the_results(): lax.ppermute(s_next, axis_name, [(pp, (pp + i0) % arr_out) for pp in rang...]
    unnamed x12 -> x2, local copies, waits for them, and re-layouts: 12.3 us -> 3.92 us
    ppermute x0 -> x3, starting transfers between devices: none -> 6.22 us  [finish_the_results(): lax.ppermute(s_next, axis_name, [(pp, (pp + i0) % arr_out) for pp in rang...]
    concatenate x0 -> x1, local copies, waits for them, and re-layouts: none -> 5.95 us  [finish_the_results(): jnp.roll(jnp.concatenate(leaves[::-1], axis=0), (formed + 1) * leaves[0]....]
    all_to_all x1 -> x0, local copies, waits for them, and re-layouts: 3.21 us -> none  [shards(): lax.all_to_all(qkv, 'uly', split_axis=2, concat_axis=0, tiled=True)]
    concatenate x0 -> x1, other arithmetic: none -> 2.99 us  [finish_the_results(): y = jnp.roll(message, -formed * v_next, 2)]
    ppermute x0 -> x3, local copies, waits for them, and re-layouts: none -> 2.43 us  [finish_the_results(): lax.ppermute(s_next, axis_name, [(pp, (pp + i0) % arr_out) for pp in rang...]
  transfers between devices with their start and end apart: 1 -> 4, of which waited for: 1 -> 3; matrix products, arithmetic and copies ran while one was open for 2% -> 4% of each run, Pallas kernels for 0% -> 0%
where the time goes in v1:
time: 62.8 us; the launch traced here: 62.4 us
  waiting for transfers between devices  34.8 us (55%)
  local copies, waits for them, and re-layouts  14.9 us (24%)
  starting transfers between devices  6.23 us (10%)
  other arithmetic  4.07 us (6%)
  matrix products  1.67 us (3%)
  between operations  0.78 us (1%)
    ppermute x3, waiting for transfers between devices, finish_the_results(): lax.ppermute(s_next, axis_name, [(pp, (pp + i0) % arr_out) for pp in rang...  23.2 us
    ppermute x1, waiting for transfers between devices, from_behind(): return lax.ppermute(value, axis, pairs)  11.6 us
    ppermute x3, starting transfers between devices, finish_the_results(): lax.ppermute(s_next, axis_name, [(pp, (pp + i0) % arr_out) for pp in rang...  6.22 us
    concatenate x1, local copies, waits for them, and re-layouts, finish_the_results(): jnp.roll(jnp.concatenate(leaves[::-1], axis=0), (formed + 1) * leaves[0]....  5.95 us
    unnamed x2, local copies, waits for them, and re-layouts  3.92 us
    concatenate x1, other arithmetic, finish_the_results(): y = jnp.roll(message, -formed * v_next, 2)  2.99 us
    ppermute x3, local copies, waits for them, and re-layouts, finish_the_results(): lax.ppermute(s_next, axis_name, [(pp, (pp + i0) % arr_out) for pp in rang...  2.43 us
  transfers between devices with their start and end apart: 4, of which 3 were waited for; matrix products, arithmetic and copies ran while one was open for 4% of the time, Pallas kernels for 0%

profile of v1, /device:TPU:0, one launch (start us, length us, event | category | flops | bytes accessed | tf_op | source)
XLA Modules:
  0.0 62.4 jit_solution(17585784282270770420)
XLA Ops:
  0.7 2.8 %copy.17 = bf16[64,3,3072]{0,2,1:T(8,128)(2,1)S(1)} copy(bf16[64,3,3072]{2,0,1:T(8,128)(2,1)} %param.1) | data formatting | bytes 2359296 | tf_op args[0]
  3.4 3.0 %fusion = bf16[64,3,3072]{0,2,1:T(8,128)(2,1)S(1)} fusion(s32[]{:T(128)S(6)} %select_n.24, bf16[64,3,3072]{0,2,1:T(8,128)(2,1)S(1)} %copy.17), kind=kLoop, calls=%fused_computation.2 | loop fusion | flops 2359296 | bytes 2359300 | tf_op jit(solution)/shard_map/jit(_roll_dynamic)/concatenate | solution.py:14
  6.4 0.2 fusion.14
  6.6 0.2 copy.19
  6.8 5.1 %collective-permute-start = (bf16[64,3,768]{2,0,1:T(8,128)(2,1)S(1)}, bf16[64,3,768]{2,0,1:T(8,128)(2,1)S(1)}, u32[]{:S(2)}, u32[]{:S(2)}) collective-permute-start(bf16[64,3,768]{2,0,1:T(8,128)(2,1)S(1)} %copy.19), channel_id=1, source_target_pairs={{0,3},{1,0},{2,1},{3,2},{4,7},{5,4},{6,5},{7,6},{8,11},{9,8},{10,9... | collective-permute-start | bytes 884744 | tf_op jit(solution)/shard_map/ppermute | solution.py:19
  11.9 0.2 copy.20
  12.2 0.1 collective-permute-start.1
  12.2 0.2 copy.21
  12.5 1.1 %collective-permute-start.2 = (bf16[64,3,768]{2,0,1:T(8,128)(2,1)S(1)}, bf16[64,3,768]{2,0,1:T(8,128)(2,1)S(1)}, u32[]{:S(2)}, u32[]{:S(2)}) collective-permute-start(bf16[64,3,768]{2,0,1:T(8,128)(2,1)S(1)} %copy.21), channel_id=1, source_target_pairs={{0,1},{1,2},{2,3},{3,0},{4,5},{5,6},{6,7},{7,4},{8,9},{9,10},{10,1... | collective-permute-start | bytes 884744 | tf_op jit(solution)/shard_map/ppermute | solution.py:19
  13.5 5.9 %collective-permute-done = bf16[64,3,768]{2,0,1:T(8,128)(2,1)S(1)} collective-permute-done((bf16[64,3,768]{2,0,1:T(8,128)(2,1)S(1)}, bf16[64,3,768]{2,0,1:T(8,128)(2,1)S(1)}, u32[]{:S(2)}, u32[]{:S(2)}) %collective-permute-start) | collective-permute-done | bytes 294944 | tf_op jit(solution)/shard_map/ppermute | solution.py:19
  19.4 0.3 copy.22
  19.7 17.3 %collective-permute-done.1 = bf16[64,3,768]{2,0,1:T(8,128)(2,1)S(1)} collective-permute-done((bf16[64,3,768]{2,0,1:T(8,128)(2,1)S(1)}, bf16[64,3,768]{2,0,1:T(8,128)(2,1)S(1)}, u32[]{:S(2)}, u32[]{:S(2)}) %collective-permute-start.1) | collective-permute-done | bytes 294944 | tf_op jit(solution)/shard_map/ppermute | solution.py:19
  37.1 1.1 %copy.23 = bf16[64,3,768]{0,2,1:T(8,128)(2,1)} copy(bf16[64,3,768]{2,0,1:T(8,128)(2,1)S(1)} %collective-permute-done.1) | data formatting | bytes 589824 | tf_op jit(solution)/shard_map/ppermute | solution.py:19
  38.1 0.0 collective-permute-done.2
  38.1 1.1 %copy.24 = bf16[64,3,768]{0,2,1:T(8,128)(2,1)} copy(bf16[64,3,768]{2,0,1:T(8,128)(2,1)S(1)} %collective-permute-done.2) | data formatting | bytes 589824 | tf_op jit(solution)/shard_map/ppermute | solution.py:19
  39.2 5.9 %concatenate.11 = bf16[512,3,768]{0,2,1:T(8,128)(2,1)S(1)} concatenate(bf16[64,3,768]{0,2,1:T(8,128)(2,1)S(1)} %copy.22, bf16[64,3,768]{0,2,1:T(8,128)(2,1)} %copy.23, bf16[64,3,768]{0,2,1:T(8,128)(2,1)} %copy.24, bf16[64,3,768]{0,2,1:T(8,128)(2,1)S(1)} %get-tuple-element.37, bf16[64,3,768]{0,2,1:T(8,128)(2,1)S(1)} %copy.22, bf16[64,3,768]{0,2,1:T(8,128)(2,1)} %copy.23, ...), dimensions={0} | concatenate | bytes 4718592 | tf_op jit(solution)/shard_map/jit(_roll_dynamic)/concatenate | solution.py:21
  45.1 1.2 %constant_dynamic-slice_fusion.2 = bf16[256,2,768]{0,2,1:T(8,128)(2,1)} fusion(bf16[512,3,768]{0,2,1:T(8,128)(2,1)S(1)} %concatenate.11, s32[]{:T(128)S(6)} %select_n.26, s32[]{:T(128)S(6)} %add.56), kind=kLoop, calls=%fused_computation.25 | loop fusion | bytes 1572872 | tf_op jit(solution)/shard_map/slice | solution.py:71
  46.3 0.0 collective-permute-start.3
  46.3 0.5 constant_dynamic-slice_fusion.1
  46.8 0.4 fusion.16
  47.2 11.6 %collective-permute-done.3 = bf16[256,2,768]{0,2,1:T(8,128)(2,1)S(1)} collective-permute-done((bf16[256,2,768]{0,2,1:T(8,128)(2,1)}, bf16[256,2,768]{0,2,1:T(8,128)(2,1)S(1)}, u32[]{:S(2)}, u32[]{:S(2)}) %collective-permute-start.3) | collective-permute-done | bytes 786464 | tf_op jit(solution)/shard_map/ppermute | solution.py:32
  58.9 0.1 fusion.15
  58.9 0.4 fusion.17
  59.4 0.4 fusion.1
  59.8 0.6 log_add_fusion
  60.4 0.4 convolution_bitcast_fusion
  60.9 0.4 fusion.7
  61.3 1.1 %copy.34 = f32[256,768]{1,0:T(8,128)} copy(f32[256,768]{0,1:T(8,128)S(1)} %bitcast.39) | data formatting | bytes 1572864
  (2 shorter events, 0.0 us)
Async XLA Ops:
  6.8 12.6 %collective-permute-start = (bf16[64,3,768]{2,0,1:T(8,128)(2,1)S(1)}, bf16[64,3,768]{2,0,1:T(8,128)(2,1)S(1)}, u32[]{:S(2)}, u32[]{:S(2)}) collective-permute-start(bf16[64,3,768]{2,0,1:T(8,128)(2,1)S(1)} %copy.19), channel_id=1, source_target_pairs={{0,3},{1,0},{2,1},{3,2},{4,7},{5,4},{6,5},{7,6},{8,11},{9,8},{10,9... | collective-permute-start | bytes 884744 | tf_op jit(solution)/shard_map/ppermute | solution.py:19
  12.2 24.9 %collective-permute-start.1 = (bf16[64,3,768]{2,0,1:T(8,128)(2,1)S(1)}, bf16[64,3,768]{2,0,1:T(8,128)(2,1)S(1)}, u32[]{:S(2)}, u32[]{:S(2)}) collective-permute-start(bf16[64,3,768]{2,0,1:T(8,128)(2,1)S(1)} %copy.20), channel_id=1, source_target_pairs={{0,2},{1,3},{2,0},{3,1},{4,6},{5,7},{6,4},{7,5},{8,10},{9,11},{10,... | collective-permute-start | bytes 884744 | tf_op jit(solution)/shard_map/ppermute | solution.py:19
  12.5 25.6 %collective-permute-start.2 = (bf16[64,3,768]{2,0,1:T(8,128)(2,1)S(1)}, bf16[64,3,768]{2,0,1:T(8,128)(2,1)S(1)}, u32[]{:S(2)}, u32[]{:S(2)}) collective-permute-start(bf16[64,3,768]{2,0,1:T(8,128)(2,1)S(1)} %copy.21), channel_id=1, source_target_pairs={{0,1},{1,2},{2,3},{3,0},{4,5},{5,6},{6,7},{7,4},{8,9},{9,10},{10,1... | collective-permute-start | bytes 884744 | tf_op jit(solution)/shard_map/ppermute | solution.py:19
  46.3 12.5 %collective-permute-start.3 = (bf16[256,2,768]{0,2,1:T(8,128)(2,1)}, bf16[256,2,768]{0,2,1:T(8,128)(2,1)S(1)}, u32[]{:S(2)}, u32[]{:S(2)}) collective-permute-start(bf16[256,2,768]{0,2,1:T(8,128)(2,1)} %constant_dynamic-slice_fusion.2), channel_id=1, source_target_pairs={{0,4},{4,8},{8,12},{12,16},{16,20},{20,24},{24,28},{28,0},{1,5},{5... | collective-permute-start | bytes 2359304 | tf_op jit(solution)/shard_map/ppermute | solution.py:32
